TPU v7x, 32 devices: a whole 2x2x4 slice. The times are simulated.
32 devices in a mesh: frames: 2 (over x), chain: 16 (over z, y, core).
Axes of the slice: x: 2, y: 2, z: 4, core: 2. Of those that a mesh axis runs over, the one named last changes fastest.
Arguments:
- species: int32 [8192], P(('frames', 'chain')), parts along dimension 0, may hold values from 0 to 127
- positions: float32 [3, 8192], P(None, ('frames', 'chain')), parts along dimension 1, may hold values from -18 to 18
- block_list: int32 [64, 3], P(('frames', 'chain')), parts along dimension 0, may hold values from -1 to 31, as said below
- embed_table: bfloat16 [128, 512], replicated, may hold values from -6 to 6
- w_query: bfloat16 [2, 512, 512], replicated, may hold values from -0.25 to 0.25
- w_key: bfloat16 [2, 512, 512], replicated, may hold values from -0.25 to 0.25
- w_value: bfloat16 [2, 512, 512], replicated, may hold values from -0.25 to 0.25
- w_out: bfloat16 [2, 512, 512], replicated, may hold values from -0.25 to 0.25
- w_up: bfloat16 [2, 512, 1024], replicated, may hold values from -0.25 to 0.25
- w_down: bfloat16 [2, 1024, 512], replicated, may hold values from -0.1875 to 0.1875
- norm_gains: float32 [2, 2, 512], replicated, may hold values from 0.5 to 1.5
- gammas: float32 [2, 16], replicated, may hold values from 0.005 to 0.1
- out_gain: float32 [512], replicated, may hold values from 0.5 to 1.5
- readout: float32 [512], replicated, may hold values from -0.25 to 0.25
Outputs:
- energy: float32 [2], P('frames'), parts along dimension 0
- forces: float32 [3, 8192], P(None, ('frames', 'chain')), parts along dimension 1
There are 2 independent parts, one for each index of `frames`. A program takes and returns all parts, laid end to end along the dimension named above; an argument that names none is the same for every part. Nothing has to cross between parts.
Inputs may be any that keep to these rules, and one draw needn't show every extreme that they name: `block_list`: row b holds b-1 or -1, then b, then b+1 or -1; -1 marks a neighbouring block outside the cutoff.
All inputs are finite; a program needn't handle non-finite values.
Results may differ from a plain program's by a relative error of at most 0.022.
Values may be sent and summed in bfloat16 or wider, within the bound.
A program may use at most 128 MiB of HBM per device.

v0:
```python
from functools import partial

import jax
import jax.numpy as jnp
from jax import lax
from jax.sharding import PartitionSpec as P

BLOCK = 128


def padded(block, sides, width):
    for axis, dim in sides:
        count = lax.axis_size(axis)
        forward = [(i, i + 1) for i in range(count - 1)]
        backward = [(target, source) for source, target in forward]
        low = lax.ppermute(
            lax.slice_in_dim(block, block.shape[dim] - width, None, axis=dim), axis, forward
        )
        high = lax.ppermute(lax.slice_in_dim(block, 0, width, axis=dim), axis, backward)
        block = jnp.concatenate([low, block, high], axis=dim)
    return block


def shifted(value, axis, steps):
    count = lax.axis_size(axis)
    leading, last = (max(0, -steps), min(count, count - steps))
    return lax.ppermute(value, axis, [(source, source + steps) for source in range(leading, last)])


def rms(x, gain):
    return x * lax.rsqrt(jnp.mean(x * x, axis=-1, keepdims=True) + 1e-06) * gain


def windows(ext, nblk):
    blocks = ext.reshape(nblk + 2, 128, ext.shape[-1])
    return jnp.concatenate([blocks[:-2], blocks[1:-1], blocks[2:]], axis=1)


def attend(query, key_ext, value_ext, coord, coord_ext, valid, gamma, heads):
    atoms, width = query.shape
    nblk = atoms // 128
    hdim = width // heads
    key_win = windows(key_ext, nblk).astype(jnp.bfloat16).reshape(nblk, 384, heads, hdim)
    value_win = windows(value_ext, nblk).astype(jnp.bfloat16).reshape(nblk, 384, heads, hdim)
    query_blk = query.reshape(nblk, 128, heads, hdim)
    scores = jnp.einsum(
        "bqhd,bkhd->bhqk", query_blk, key_win, preferred_element_type=jnp.float32
    ) * hdim ** (-0.5)
    coord_blk = coord_ext.reshape(3, nblk + 2, 128)
    coord_win = jnp.concatenate([coord_blk[:, :-2], coord_blk[:, 1:-1], coord_blk[:, 2:]], axis=2)
    coord_q = coord.reshape(3, nblk, 128)
    dist_sq = jnp.sum((coord_q[:, :, :, None] - coord_win[:, :, None, :]) ** 2, axis=0)
    scores = scores - gamma[None, :, None, None] * dist_sq[:, None]
    keymask = jnp.repeat(valid, 128, axis=1)
    scores = jnp.where(keymask[:, None, None, :], scores, -1e30)
    peak = lax.stop_gradient(jnp.max(scores, axis=-1, keepdims=True))
    expo = jnp.exp(scores - peak)
    probs = (expo / jnp.sum(expo, axis=-1, keepdims=True)).astype(jnp.bfloat16)
    mixed = jnp.einsum("bhqk,bkhd->bqhd", probs, value_win, preferred_element_type=jnp.float32)
    return mixed.reshape(atoms, width).astype(jnp.bfloat16)


def finish(weights, valid, state, query, key_ext, value_ext, coord, coord_ext):
    att = attend(
        query, key_ext, value_ext, coord, coord_ext, valid, weights[7], weights[7].shape[0]
    )
    state = state + jnp.dot(att, weights[3], preferred_element_type=jnp.float32)
    inner = rms(state, weights[6][1]).astype(jnp.bfloat16)
    hidden = jax.nn.gelu(jnp.dot(inner, weights[4], preferred_element_type=jnp.float32)).astype(
        jnp.bfloat16
    )
    return state + jnp.dot(hidden, weights[5], preferred_element_type=jnp.float32)


def payload_inputs(state, weights):
    return rms(state, weights[6][0]).astype(jnp.bfloat16)


def mix_inputs(
    weights, valid, state, coord, coord_low, coord_high, normed_own, normed_low, normed_high
):
    query = jnp.dot(
        normed_own.astype(jnp.bfloat16), weights[0], preferred_element_type=jnp.float32
    ).astype(jnp.bfloat16)
    normed_ext = jnp.concatenate([normed_low, normed_own, normed_high], axis=0).astype(jnp.bfloat16)
    key_ext = (
        jnp.dot(normed_ext, weights[1], preferred_element_type=jnp.float32)
        .astype(jnp.bfloat16)
        .astype(jnp.float32)
    )
    value_ext = (
        jnp.dot(normed_ext, weights[2], preferred_element_type=jnp.float32)
        .astype(jnp.bfloat16)
        .astype(jnp.float32)
    )
    coord_ext = jnp.concatenate([coord_low, coord, coord_high], axis=1)
    return finish(weights, valid, state, query, key_ext, value_ext, coord, coord_ext)


def place_first(rows, atoms):
    return jnp.pad(rows, ((0, atoms - rows.shape[0]), (0, 0)))


def place_last(rows, atoms):
    return jnp.pad(rows, ((atoms - rows.shape[0], 0), (0, 0)))


def energy_local(state, out_gain, readout):
    return jnp.sum(jnp.dot(rms(state, out_gain), readout, precision=lax.Precision.HIGHEST))


def local(
    species,
    positions,
    block_list,
    embed_table,
    w_query,
    w_key,
    w_value,
    w_out,
    w_up,
    w_down,
    norm_gains,
    gammas,
    out_gain,
    readout,
):
    atoms = species.shape[0]
    nblk = atoms // BLOCK
    width = embed_table.shape[1]
    layers = w_query.shape[0]
    ids = lax.axis_index("chain") * nblk + jnp.arange(nblk, dtype=jnp.int32)
    expect = ids[:, None] - 1 + jnp.arange(3, dtype=jnp.int32)[None, :]
    valid = (block_list == expect) & (block_list >= 0)
    coord_ext = padded(positions, (("chain", 1),), BLOCK)
    coord_low = coord_ext[:, :BLOCK]
    coord_high = coord_ext[:, -BLOCK:]
    onehot = jax.nn.one_hot(species, embed_table.shape[0], dtype=jnp.bfloat16)
    state = jnp.dot(onehot, embed_table, preferred_element_type=jnp.float32)
    saved = []
    for layer in range(layers):
        weights = (
            w_query[layer],
            w_key[layer],
            w_value[layer],
            w_out[layer],
            w_up[layer],
            w_down[layer],
            norm_gains[layer],
            gammas[layer],
        )
        normed = payload_inputs(state, weights)
        normed_ext = padded(normed, (("chain", 0),), BLOCK)
        rims = (
            normed.astype(jnp.float32),
            normed_ext[:BLOCK].astype(jnp.float32),
            normed_ext[-BLOCK:].astype(jnp.float32),
        )
        layer_fn = partial(mix_inputs, weights, valid)
        saved.append((state, rims, weights))
        state = layer_fn(state, positions, coord_low, coord_high, *rims)
    local_total, pullback = jax.vjp(lambda final: energy_local(final, out_gain, readout), state)
    energy = lax.psum(local_total, "chain").reshape(1)
    (grad_state,) = pullback(jnp.ones((), jnp.float32))
    grad_coord = jnp.zeros_like(positions)
    span = BLOCK * width
    for layer in reversed(range(layers)):
        state_in, rims, weights = saved[layer]
        layer_fn = partial(mix_inputs, weights, valid)
        _, layer_pull = jax.vjp(layer_fn, state_in, positions, coord_low, coord_high, *rims)
        (
            grad_mix,
            grad_pos,
            gradient_position_lower_band,
            gradient_position_upper_band,
            grad_nown,
            grad_nlow,
            grad_nhigh,
        ) = layer_pull(grad_state)
        packed_low = jnp.concatenate(
            [grad_nlow.reshape(-1), gradient_position_lower_band.reshape(-1)]
        )
        packed_high = jnp.concatenate(
            [grad_nhigh.reshape(-1), gradient_position_upper_band.reshape(-1)]
        )
        from_after = shifted(packed_low.astype(jnp.bfloat16), "chain", -1).astype(packed_low.dtype)
        from_before = shifted(packed_high.astype(jnp.bfloat16), "chain", 1).astype(
            packed_high.dtype
        )
        grad_nown = (
            grad_nown
            + place_last(from_after[:span].reshape(BLOCK, width), atoms)
            + place_first(from_before[:span].reshape(BLOCK, width), atoms)
        )
        coordinate_following = from_after[span:].reshape(3, BLOCK)
        coord_before = from_before[span:].reshape(3, BLOCK)
        _, own_pull = jax.vjp(lambda inner: payload_inputs(inner, weights), state_in)
        (grad_own,) = own_pull(grad_nown.astype(jnp.bfloat16))
        grad_coord = (
            grad_coord
            + grad_pos
            + jnp.pad(coordinate_following, ((0, 0), (atoms - BLOCK, 0)))
            + jnp.pad(coord_before, ((0, 0), (0, atoms - BLOCK)))
        )
        grad_state = grad_mix + grad_own
    return (energy, -grad_coord)


def solution(mesh):
    return jax.shard_map(
        local,
        mesh=mesh,
        in_specs=(
            P(("frames", "chain")),
            P(None, ("frames", "chain")),
            P(("frames", "chain"), None),
            P(),
            P(),
            P(),
            P(),
            P(),
            P(),
            P(),
            P(),
            P(),
            P(),
            P(),
        ),
        out_specs=(P("frames"), P(None, ("frames", "chain"))),
        check_vma=False,
    )
```

profile of v0, /device:TPU:1, one launch (start us, length us, event | category | flops | bytes accessed | tf_op | source)
XLA Modules:
  0.0 241.6 jit_solution(14874150779433154821)
XLA Ops:
  1.4 4.5 %collective-permute-start.2 = (f32[3,128]{1,0:T(4,128)S(1)}, f32[3,128]{1,0:T(4,128)S(1)}, u32[]{:S(2)}, u32[]{:S(2)}) collective-permute-start(f32[3,128]{1,0:T(4,128)S(1)} %get-tuple-element.59), channel_id=1, source_target_pairs={{0,1},{1,2},{2,3},{3,4},{4,5},{5,6},{6,7},{7,8},{8,9},{9,10},{10,1... | collective-permute-start | bytes 4616 | tf_op jit(solution)/shard_map/ppermute | solution.py:16
  5.9 1.9 collective-permute-start.3
  10.6 3.6 %collective-permute-start = (bf16[128,512]{1,0:T(8,128)(2,1)S(1)}, bf16[128,512]{1,0:T(8,128)(2,1)S(1)}, u32[]{:S(2)}, u32[]{:S(2)}) collective-permute-start(bf16[128,512]{1,0:T(8,128)(2,1)S(1)} %get-tuple-element.40), channel_id=1, source_target_pairs={{0,1},{1,2},{2,3},{3,4},{4,5},{5,6},{6,7},{7,8},{8,9},{9,10},{10,1... | collective-permute-start | bytes 393224 | tf_op jit(solution)/shard_map/ppermute | solution.py:16
  14.3 1.9 collective-permute-start.1
  21.8 1.6 convolution_convert_fusion.11
  28.8 5.0 %fusion.301 = (f32[2,16,128]{2,1,0:T(8,128)S(1)}, f32[2,16,128,384]{3,2,1,0:T(8,128)}) fusion(f32[2,128,384]{2,1,0:T(8,128)S(1)} %fusion.62, f32[16]{0:T(128)S(1)} %get-tuple-element.64, pred[2,384]{1,0:T(4,128)(4,1)S(1)} %bitcast.297, bf16[2,128,16,32]{1,3,2,0:T(8,128)(2,1)S(1)} %copy.101, bf16[2,128,16,32]{1,3,2,0:T(8,128)(2,1)S(1)} %copy.100, ...), kind=kOutput, calls=%fused_computation.385 | convolution fusion | flops 112460160 | bytes 7750464 | tf_op jit(solution)/shard_map/sub | solution.py:57
  33.9 3.4 %divide_convert_fusion.1 = bf16[2,16,128,384]{3,2,1,0:T(8,128)(2,1)S(1)} fusion(f32[2,16,128,384]{3,2,1,0:T(8,128)} %get-tuple-element.68, f32[2,16,128]{2,1,0:T(8,128)S(1)} %get-tuple-element.67), kind=kLoop, calls=%fused_computation.23 | loop fusion | flops 3145728 | bytes 9453568 | tf_op jit(solution)/shard_map/convert_element_type | solution.py:58
  37.3 2.5 %fusion.66 = bf16[2,128,16,32]{1,3,2,0:T(8,128)(2,1)S(1)} fusion(bf16[2,384,16,32]{1,3,2,0:T(8,128)(2,1)} %copy_dynamic-update-slice_fusion.6, bf16[2,16,128,384]{3,2,1,0:T(8,128)(2,1)S(1)} %divide_convert_fusion.1), kind=kOutput, calls=%fused_computation.104 | convolution fusion | flops 100794368 | bytes 4194304 | tf_op jit(solution)/shard_map/bhqk,bkhd->bqhd/dot_general | solution.py:59
  45.9 3.6 %collective-permute-start.4 = (bf16[128,512]{1,0:T(8,128)(2,1)}, bf16[128,512]{1,0:T(8,128)(2,1)S(1)}, u32[]{:S(2)}, u32[]{:S(2)}) collective-permute-start(bf16[128,512]{1,0:T(8,128)(2,1)} %get-tuple-element.38), channel_id=1, source_target_pairs={{0,1},{1,2},{2,3},{3,4},{4,5},{5,6},{6,7},{7,8},{8,9},{9,10},{10,1... | collective-permute-start | bytes 393224 | tf_op jit(solution)/shard_map/ppermute | solution.py:16
  49.5 2.1 collective-permute-start.5
  52.3 3.8 %collective-permute-done.5 = bf16[128,512]{1,0:T(8,128)(2,1)S(1)} collective-permute-done((bf16[128,512]{1,0:T(8,128)(2,1)}, bf16[128,512]{1,0:T(8,128)(2,1)S(1)}, u32[]{:S(2)}, u32[]{:S(2)}) %collective-permute-start.5) | collective-permute-done | bytes 131104 | tf_op jit(solution)/shard_map/ppermute | solution.py:19
  56.0 1.6 convolution_convert_fusion.9
  58.6 1.8 copy.106
  60.4 1.7 concatenate.100
  62.1 1.8 copy.105
  63.9 1.7 concatenate.99
  65.6 1.8 copy.104
  67.4 1.7 concatenate.98
  69.1 1.7 convolution_convert_fusion.8
  71.8 1.8 copy.113
  73.6 1.7 concatenate.104
  75.3 1.8 copy.112
  77.1 1.7 concatenate.103
  78.8 1.8 copy.111
  80.6 1.7 concatenate.102
  82.3 1.8 copy_dynamic-update-slice_fusion.2
  84.1 1.7 copy_dynamic-update-slice_fusion.5
  85.8 1.7 copy_dynamic-update-slice_fusion.1
  87.5 1.7 copy_dynamic-update-slice_fusion
  89.2 6.2 %fusion.304 = (f32[2,16,128]{2,1,0:T(8,128)S(1)}, f32[2,16,128,384]{3,2,1,0:T(8,128)}) fusion(f32[16]{0:T(128)S(1)} %get-tuple-element.63, f32[2,128,384]{2,1,0:T(8,128)} %copy-done.28, pred[2,384]{1,0:T(4,128)(4,1)S(1)} %bitcast.298, bf16[2,384,16,32]{1,3,2,0:T(8,128)(2,1)} %copy_dynamic-update-slice_fusion, bf16[2,128,16,32]{1,0,3,2:T(2,128)(2,1)S(1)} %reshape.352), kind=kOutput, calls=%fused_computation.386 | convolution fusion | flops 110100864 | bytes 7750464 | tf_op jit(solution)/shard_map/sub | solution.py:57
  95.5 3.4 %divide_convert_fusion = bf16[2,16,128,384]{3,2,1,0:T(8,128)(2,1)S(1)} fusion(f32[2,16,128,384]{3,2,1,0:T(8,128)} %get-tuple-element.74, f32[2,16,128]{2,1,0:T(8,128)S(1)} %get-tuple-element.73), kind=kLoop, calls=%fused_computation.20 | loop fusion | flops 3145728 | bytes 9453568 | tf_op jit(solution)/shard_map/convert_element_type | solution.py:58
  103.5 4.2 %multiply_reduce_fusion.4 = (f32[256]{0:T(256)S(1)}, f32[256,512]{1,0:T(8,128)}) fusion(f32[256,512]{1,0:T(8,128)} %copy-done.5, f32[512]{0:T(512)S(1)} %bitcast.311, bf16[2,512,1024]{2,1,0:T(8,128)(2,1)} %param.22, f32[256,1024]{1,0:T(8,128)} %copy-done.24, bf16[2,1024,512]{2,1,0:T(8,128)(2,1)} %param.23, f32[256,512]{1,0:T(8,128)} %get-tuple-element.77, ...), kind=kOutput, calls=%fused_computation.192 | convolution fusion | flops 543555328 | bytes 4725760 | tf_op jit(solution)/shard_map/transpose(jvp())/dot_general | solution.py:69
  107.7 1.6 add_add_fusion.2
  113.4 2.7 %fusion.50 = f32[2,16,32,384]{3,2,1,0:T(8,128)S(1)} fusion(bf16[2,16,128,384]{3,2,1,0:T(8,128)(2,1)} %copy-done.2, bf16[2,16,32,128]{3,0,2,1:T(2,128)(2,1)S(1)} %bitcast.275), kind=kOutput, calls=%fused_computation.65 | convolution fusion | flops 101449728 | bytes 4980736 | tf_op jit(solution)/shard_map/transpose(jvp(bhqk,bkhd->bqhd))/dot_general | solution.py:59
  116.1 4.9 %fusion.6 = (f32[2,16,128]{2,1,0:T(8,128)S(1)}, bf16[2,16,128,384]{3,2,1,0:T(8,128)(2,1)S(1)}) fusion(f32[2,16,128,384]{3,2,1,0:T(8,128)} %get-tuple-element.74, f32[2,16,128]{2,1,0:T(8,128)S(1)} %multiply_divide_fusion.1, bf16[2,384,16,32]{1,3,2,0:T(8,128)(2,1)} %copy-done.11, bf16[2,16,32,128]{3,0,2,1:T(2,128)(2,1)S(1)} %bitcast.276), kind=kOutput, calls=%fused_computation.10 | convolution fusion | flops 108523520 | bytes 10518528 | tf_op jit(solution)/shard_map/transpose(jvp(bhqk,bkhd->bqhd))/dot_general | solution.py:59
  121.0 3.1 %multiply_reduce_fusion.1 = (f32[2,128,384]{2,1,0:T(8,128)}, f32[2,16,128,384]{3,2,1,0:T(8,128)S(1)}) fusion(f32[16]{0:T(128)S(1)} %get-tuple-element.63, f32[2,16,128,384]{3,2,1,0:T(8,128)S(1)} %bitcast.271, f32[2,16,128]{2,1,0:T(8,128)S(1)} %neg.27, f32[2,16,128]{2,1,0:T(8,128)S(1)} %get-tuple-element.73, ...), kind=kLoop, calls=%fused_computation.19 | loop fusion | flops 12484608 | bytes 16155456 | tf_op jit(solution)/shard_map/transpose(jvp())/reduce_sum | solution.py:53
  124.1 3.1 %fusion.63 = bf16[2,128,16,32]{1,3,2,0:T(8,128)(2,1)} fusion(bf16[2,384,16,32]{1,3,2,0:T(8,128)(2,1)} %copy_dynamic-update-slice_fusion, f32[2,16,128,384]{3,2,1,0:T(8,128)S(1)} %get-tuple-element.9), kind=kOutput, calls=%fused_computation.103 | convolution fusion | flops 102367232 | bytes 7340032 | tf_op jit(solution)/shard_map/transpose(jvp(bqhd,bkhd->bhqk))/dot_general | solution.py:46
  127.2 1.8 fusion.40
  130.2 2.1 copy.144
  132.3 2.0 copy.145
  134.3 2.0 copy.146
  138.4 2.6 %fusion.289 = (f32[2,128,512]{1,2,0:T(8,128)}, f32[2,128,512]{1,2,0:T(8,128)}, f32[2,128,512]{1,2,0:T(8,128)}) fusion(f32[2,384,512]{1,2,0:T(8,128)} %bitcast.274), kind=kLoop, calls=%fused_computation.373 | loop fusion | bytes 3145728 | tf_op jit(solution)/shard_map/transpose(jvp())/split | solution.py:36
  141.0 2.0 copy.147
  143.1 2.0 copy.148
  145.1 2.1 copy.149
  147.2 1.5 add_convert_fusion.2
  148.7 1.5 convolution_convert_fusion.6
  154.1 1.9 collective-permute-start.7
  156.7 2.6 %collective-permute-start.6 = (bf16[65920]{0:T(1024)(128)(2,1)}, bf16[65920]{0:T(1024)(128)(2,1)S(1)}, u32[]{:S(2)}, u32[]{:S(2)}) collective-permute-start(bf16[65920]{0:T(1024)(128)(2,1)} %pad_maximum_fusion.12), channel_id=1, source_target_pairs={{1,0},{2,1},{3,2},{4,3},{5,4},{6,5},{7,6},{8,7},{9,8},{10,9},{11,1... | collective-permute-start | bytes 395528 | tf_op jit(solution)/shard_map/ppermute | solution.py:27
  161.2 30.2 %psum.7 = f32[1]{0:T(128)} all-reduce(f32[1]{0:T(128)} %bitcast.22), channel_id=1, replica_groups=mesh['frames'=2,'chain'=16] {'chain'}, use_global_device_ids=true, to_apply=%region_11.12 | all-reduce | flops 1 | bytes 8 | tf_op jit(solution)/shard_map/psum | solution.py:163
  192.0 1.9 copy.131
  194.7 1.7 reshape.362
  197.1 1.7 reshape.363
  198.8 2.6 %multiply_reduce_fusion.3 = (f32[256]{0:T(256)S(1)}, bf16[256,512]{1,0:T(8,128)(2,1)}) fusion(f32[256,512]{1,0:T(8,128)} %copy-done.6, f32[512]{0:T(512)} %bitcast.294, f32[128,512]{1,0:T(8,128)} %reshape.363, f32[128,512]{1,0:T(8,128)} %reshape.362, bf16[2,512,512]{2,1,0:T(8,128)(2,1)} %param.18, bf16[64,8,2,128]{3,2,1,0:T(2,128)(2,1)} %bitcast.290, ...), kind=kOutput, calls=%fused_computation.189 | convolution fusion | flops 135659264 | bytes 2362368 | tf_op jit(solution)/shard_map/transpose(jvp())/dot_general | solution.py:82
  202.1 4.5 %multiply_reduce_fusion.2 = (f32[256]{0:T(256)S(1)}, f32[256,512]{1,0:T(8,128)}) fusion(f32[256,512]{1,0:T(8,128)} %copy-done.9, f32[512]{0:T(512)} %bitcast.309, bf16[2,512,1024]{2,1,0:T(8,128)(2,1)} %param.22, f32[256,1024]{1,0:T(8,128)} %copy-done.23, bf16[2,1024,512]{2,1,0:T(8,128)(2,1)} %param.23, f32[256,512]{1,0:T(8,128)} %copy-done.8, ...), kind=kOutput, calls=%fused_computation.186 | convolution fusion | flops 543948544 | bytes 5512192 | tf_op jit(solution)/shard_map/transpose(jvp())/dot_general | solution.py:69
  206.7 2.2 convolution_convert_fusion.21
  211.5 5.1 %fusion.11 = (f32[2,16,128]{2,1,0:T(8,128)S(1)}, bf16[2,16,128,384]{3,2,1,0:T(8,128)(2,1)S(1)}) fusion(f32[2,16,128,384]{3,2,1,0:T(8,128)} %get-tuple-element.68, f32[2,16,128]{2,1,0:T(8,128)S(1)} %copy-done.36, bf16[2,384,16,32]{1,3,2,0:T(8,128)(2,1)} %copy_dynamic-update-slice_fusion.6, bf16[2,16,32,128]{3,0,2,1:T(2,128)(2,1)S(1)} %bitcast.278), kind=kOutput, calls=%fused_computation.15 | convolution fusion | flops 108523520 | bytes 10518528 | tf_op jit(solution)/shard_map/transpose(jvp(bhqk,bkhd->bqhd))/dot_general | solution.py:59
  216.6 2.3 multiply_reduce_fusion
  219.0 3.2 %fusion.46 = f32[2,16,384,32]{2,3,1,0:T(8,128)} fusion(bf16[2,128,16,32]{1,0,3,2:T(2,128)(2,1)S(1)} %copy-done.30, f32[2,16,128,384]{3,2,1,0:T(8,128)S(1)} %bitcast.269, bf16[2,16,128,384]{3,2,1,0:T(8,128)(2,1)S(1)} %get-tuple-element.87, f32[2,16,128]{2,1,0:T(8,128)S(1)} %neg.30, f32[2,16,128]{2,1,0:T(8,128)S(1)} %copy-done.32, ...), kind=kOutput, calls=%fused_computation.61 | convolution fusion | flops 110886912 | bytes 11305728 | tf_op jit(solution)/shard_map/transpose(jvp(bqhd,bkhd->bhqk))/dot_general | solution.py:46
  223.5 2.3 fusion.287
  229.4 1.5 convolution_convert_fusion.4
  232.8 1.9 collective-permute-start.9
  234.7 4.6 %collective-permute-start.8 = (bf16[65920]{0:T(1024)(128)(2,1)S(1)}, bf16[65920]{0:T(1024)(128)(2,1)S(1)}, u32[]{:S(2)}, u32[]{:S(2)}) collective-permute-start(bf16[65920]{0:T(1024)(128)(2,1)S(1)} %pad_maximum_fusion.14), channel_id=1, source_target_pairs={{1,0},{2,1},{3,2},{4,3},{5,4},{6,5},{7,6},{8,7},{9,8},{10,9},{11,1... | collective-permute-start | bytes 395528 | tf_op jit(solution)/shard_map/ppermute | solution.py:27
  239.3 1.7 collective-permute-done.8
  (267 shorter events, 53.4 us)
Async XLA Ops:
  0.6 8.0 %copy-start = (bf16[128,512]{1,0:T(8,128)(2,1)S(1)}, bf16[128,512]{1,0:T(8,128)(2,1)}, u32[]{:S(2)}) copy-start(bf16[128,512]{1,0:T(8,128)(2,1)} %param.17) | copy-start | bytes 393220
  1.4 19.5 %collective-permute-start.2 = (f32[3,128]{1,0:T(4,128)S(1)}, f32[3,128]{1,0:T(4,128)S(1)}, u32[]{:S(2)}, u32[]{:S(2)}) collective-permute-start(f32[3,128]{1,0:T(4,128)S(1)} %get-tuple-element.59), channel_id=1, source_target_pairs={{0,1},{1,2},{2,3},{3,4},{4,5},{5,6},{6,7},{7,8},{8,9},{9,10},{10,1... | collective-permute-start | bytes 4616 | tf_op jit(solution)/shard_map/ppermute | solution.py:16
  5.9 15.0 %collective-permute-start.3 = (f32[3,128]{1,0:T(4,128)S(1)}, f32[3,128]{1,0:T(4,128)S(1)}, u32[]{:S(2)}, u32[]{:S(2)}) collective-permute-start(f32[3,128]{1,0:T(4,128)S(1)} %get-tuple-element.60), channel_id=1, source_target_pairs={{1,0},{2,1},{3,2},{4,3},{5,4},{6,5},{7,6},{8,7},{9,8},{10,9},{11,1... | collective-permute-start | bytes 4616 | tf_op jit(solution)/shard_map/ppermute | solution.py:19
  8.6 31.9 %copy-start.52 = (f32[1,1,512]{2,1,0:T(1,128)}, f32[1,1,512]{2,1,0:T(1,128)S(1)}, u32[]{:S(2)}) copy-start(f32[1,1,512]{2,1,0:T(1,128)S(1)} %get-tuple-element.49) | copy-start | bytes 6148
  8.6 33.1 %copy-start.40 = (f32[1,1,512]{2,1,0:T(1,128)}, f32[1,1,512]{2,1,0:T(1,128)S(1)}, u32[]{:S(2)}) copy-start(f32[1,1,512]{2,1,0:T(1,128)S(1)} %get-tuple-element.51) | copy-start | bytes 6148
  10.6 11.2 %collective-permute-start = (bf16[128,512]{1,0:T(8,128)(2,1)S(1)}, bf16[128,512]{1,0:T(8,128)(2,1)S(1)}, u32[]{:S(2)}, u32[]{:S(2)}) collective-permute-start(bf16[128,512]{1,0:T(8,128)(2,1)S(1)} %get-tuple-element.40), channel_id=1, source_target_pairs={{0,1},{1,2},{2,3},{3,4},{4,5},{5,6},{6,7},{7,8},{8,9},{9,10},{10,1... | collective-permute-start | bytes 393224 | tf_op jit(solution)/shard_map/ppermute | solution.py:16
  14.3 7.5 %collective-permute-start.1 = (bf16[128,512]{1,0:T(8,128)(2,1)S(1)}, bf16[128,512]{1,0:T(8,128)(2,1)S(1)}, u32[]{:S(2)}, u32[]{:S(2)}) collective-permute-start(bf16[128,512]{1,0:T(8,128)(2,1)S(1)} %get-tuple-element.41), channel_id=1, source_target_pairs={{1,0},{2,1},{3,2},{4,3},{5,4},{6,5},{7,6},{8,7},{9,8},{10,9},{11,1... | collective-permute-start | bytes 393224 | tf_op jit(solution)/shard_map/ppermute | solution.py:19
  17.0 11.8 %copy-start.54 = (f32[16]{0:T(128)}, f32[16]{0:T(128)S(1)}, u32[]{:S(2)}) copy-start(f32[16]{0:T(128)S(1)} %get-tuple-element.64) | copy-start | bytes 196
  19.9 117.5 %copy-start.37 = (f32[3,2,128]{2,1,0:T(2,128)}, f32[3,2,128]{2,1,0:T(2,128)S(1)}, u32[]{:S(2)}) copy-start(f32[3,2,128]{2,1,0:T(2,128)S(1)} %sub.27) | copy-start | bytes 9220
  19.9 101.1 %copy-start.42 = (pred[1,2,3,128]{3,1,2,0:T(4,128)(4,1)}, pred[1,2,3,128]{3,1,2,0:T(4,128)(4,1)S(1)}, u32[]{:S(2)}) copy-start(pred[1,2,3,128]{3,1,2,0:T(4,128)(4,1)S(1)} %copy.238) | copy-start | bytes 2308
  20.1 8.7 %copy-start.29 = (bf16[2,128,16,32]{1,0,3,2:T(2,128)(2,1)}, bf16[2,128,16,32]{1,0,3,2:T(2,128)(2,1)S(1)}, u32[]{:S(2)}) copy-start(bf16[2,128,16,32]{1,0,3,2:T(2,128)(2,1)S(1)} %reshape.350) | copy-start | bytes 786436
  21.6 115.8 %copy-start.33 = (f32[3,2,384]{2,1,0:T(2,128)}, f32[3,2,384]{2,1,0:T(2,128)S(1)}, u32[]{:S(2)}) copy-start(f32[3,2,384]{2,1,0:T(2,128)S(1)} %pad_maximum_fusion.16) | copy-start | bytes 27652
  21.8 7.0 %copy-start.28 = (f32[2,128,384]{2,1,0:T(8,128)}, f32[2,128,384]{2,1,0:T(8,128)S(1)}, u32[]{:S(2)}) copy-start(f32[2,128,384]{2,1,0:T(8,128)S(1)} %fusion.62) | copy-start | bytes 1179652
  33.8 17.8 %copy-start.31 = (f32[2,16,128]{2,1,0:T(8,128)}, f32[2,16,128]{2,1,0:T(8,128)S(1)}, u32[]{:S(2)}) copy-start(f32[2,16,128]{2,1,0:T(8,128)S(1)} %get-tuple-element.67) | copy-start | bytes 49156
  33.9 6.2 %copy-start.4 = (f32[256,512]{1,0:T(8,128)S(1)}, f32[256,512]{1,0:T(8,128)}, u32[]{:S(2)}) copy-start(f32[256,512]{1,0:T(8,128)} %copy-done.3) | copy-start | bytes 1572868
  33.9 6.2 %copy-start.12 = (bf16[2,512,512]{2,1,0:T(8,128)(2,1)S(1)}, bf16[2,512,512]{2,1,0:T(8,128)(2,1)}, u32[]{:S(2)}) copy-start(bf16[2,512,512]{2,1,0:T(8,128)(2,1)} %param.21) | copy-start | bytes 3145732
  33.9 6.6 %copy-start.15 = (bf16[2,512,1024]{2,1,0:T(8,128)(2,1)S(1)}, bf16[2,512,1024]{2,1,0:T(8,128)(2,1)}, u32[]{:S(2)}) copy-start(bf16[2,512,1024]{2,1,0:T(8,128)(2,1)} %param.22) | copy-start | bytes 6291460
  37.2 3.8 %copy-start.56 = (bf16[2,1024,512]{2,1,0:T(8,128)(2,1)S(1)}, bf16[2,1024,512]{2,1,0:T(8,128)(2,1)}, u32[]{:S(2)}) copy-start(bf16[2,1024,512]{2,1,0:T(8,128)(2,1)} %param.23) | copy-start | bytes 6291460
  37.2 5.3 %copy-start.58 = (bf16[2,512,512]{2,1,0:T(8,128)(2,1)S(1)}, bf16[2,512,512]{2,1,0:T(8,128)(2,1)}, u32[]{:S(2)}) copy-start(bf16[2,512,512]{2,1,0:T(8,128)(2,1)} %param.18) | copy-start | bytes 3145732
  40.5 17.2 %copy-start.46 = (f32[256]{0:T(256)}, f32[256]{0:T(256)S(1)}, u32[]{:S(2)}) copy-start(f32[256]{0:T(256)S(1)} %fusion.241) | copy-start | bytes 3076
  41.7 29.2 %copy-start.53 = (f32[256]{0:T(256)}, f32[256]{0:T(256)S(1)}, u32[]{:S(2)}) copy-start(f32[256]{0:T(256)S(1)} %get-tuple-element.71) | copy-start | bytes 3076
  41.7 29.2 %copy-start.48 = (f32[256]{0:T(256)}, f32[256]{0:T(256)S(1)}, u32[]{:S(2)}) copy-start(f32[256]{0:T(256)S(1)} %fusion.242) | copy-start | bytes 3076
  45.9 43.3 %copy-start.21 = (bf16[2,128,16,32]{1,0,3,2:T(2,128)(2,1)}, bf16[2,128,16,32]{1,0,3,2:T(2,128)(2,1)S(1)}, u32[]{:S(2)}) copy-start(bf16[2,128,16,32]{1,0,3,2:T(2,128)(2,1)S(1)} %reshape.352) | copy-start | bytes 786436
  45.9 6.4 %collective-permute-start.4 = (bf16[128,512]{1,0:T(8,128)(2,1)}, bf16[128,512]{1,0:T(8,128)(2,1)S(1)}, u32[]{:S(2)}, u32[]{:S(2)}) collective-permute-start(bf16[128,512]{1,0:T(8,128)(2,1)} %get-tuple-element.38), channel_id=1, source_target_pairs={{0,1},{1,2},{2,3},{3,4},{4,5},{5,6},{6,7},{7,8},{8,9},{9,10},{10,1... | collective-permute-start | bytes 393224 | tf_op jit(solution)/shard_map/ppermute | solution.py:16
  49.5 6.5 %collective-permute-start.5 = (bf16[128,512]{1,0:T(8,128)(2,1)}, bf16[128,512]{1,0:T(8,128)(2,1)S(1)}, u32[]{:S(2)}, u32[]{:S(2)}) collective-permute-start(bf16[128,512]{1,0:T(8,128)(2,1)} %get-tuple-element.39), channel_id=1, source_target_pairs={{1,0},{2,1},{3,2},{4,3},{5,4},{6,5},{7,6},{8,7},{9,8},{10,9},{11,1... | collective-permute-start | bytes 393224 | tf_op jit(solution)/shard_map/ppermute | solution.py:19
  52.3 6.3 %copy-start.59 = (bf16[128,512]{1,0:T(8,128)(2,1)}, bf16[128,512]{1,0:T(8,128)(2,1)S(1)}, u32[]{:S(2)}) copy-start(bf16[128,512]{1,0:T(8,128)(2,1)S(1)} %collective-permute-done.4) | copy-start | bytes 393220
  95.4 3.4 %copy-start.10 = (bf16[2,384,16,32]{1,3,2,0:T(8,128)(2,1)S(1)}, bf16[2,384,16,32]{1,3,2,0:T(8,128)(2,1)}, u32[]{:S(2)}) copy-start(bf16[2,384,16,32]{1,3,2,0:T(8,128)(2,1)} %copy_dynamic-update-slice_fusion.5) | copy-start | bytes 2359300
  95.5 3.4 %copy-start.26 = (bf16[2,128,16,32]{1,0,3,2:T(2,128)(2,1)S(1)}, bf16[2,128,16,32]{1,0,3,2:T(2,128)(2,1)}, u32[]{:S(2)}) copy-start(bf16[2,128,16,32]{1,0,3,2:T(2,128)(2,1)} %concatenate.99) | copy-start | bytes 786436
  95.5 3.5 %copy-start.25 = (bf16[2,128,16,32]{1,0,3,2:T(2,128)(2,1)S(1)}, bf16[2,128,16,32]{1,0,3,2:T(2,128)(2,1)}, u32[]{:S(2)}) copy-start(bf16[2,128,16,32]{1,0,3,2:T(2,128)(2,1)} %concatenate.100) | copy-start | bytes 786436
  95.5 5.1 %copy-start.7 = (f32[256,512]{1,0:T(8,128)S(1)}, f32[256,512]{1,0:T(8,128)}, u32[]{:S(2)}) copy-start(f32[256,512]{1,0:T(8,128)} %copy-done.6) | copy-start | bytes 1572868
  95.5 5.1 %copy-start.13 = (bf16[2,512,512]{2,1,0:T(8,128)(2,1)S(1)}, bf16[2,512,512]{2,1,0:T(8,128)(2,1)}, u32[]{:S(2)}) copy-start(bf16[2,512,512]{2,1,0:T(8,128)(2,1)} %param.21) | copy-start | bytes 3145732
  95.5 5.6 %copy-start.16 = (bf16[2,512,1024]{2,1,0:T(8,128)(2,1)S(1)}, bf16[2,512,1024]{2,1,0:T(8,128)(2,1)}, u32[]{:S(2)}) copy-start(bf16[2,512,1024]{2,1,0:T(8,128)(2,1)} %param.22) | copy-start | bytes 6291460
  98.9 4.5 %copy-start.2 = (bf16[2,16,128,384]{3,2,1,0:T(8,128)(2,1)}, bf16[2,16,128,384]{3,2,1,0:T(8,128)(2,1)S(1)}, u32[]{:S(2)}) copy-start(bf16[2,16,128,384]{3,2,1,0:T(8,128)(2,1)S(1)} %divide_convert_fusion) | copy-start | bytes 9437188
  98.9 3.2 %copy-start.57 = (bf16[2,1024,512]{2,1,0:T(8,128)(2,1)S(1)}, bf16[2,1024,512]{2,1,0:T(8,128)(2,1)}, u32[]{:S(2)}) copy-start(bf16[2,1024,512]{2,1,0:T(8,128)(2,1)} %param.23) | copy-start | bytes 6291460
  99.1 4.3 %copy-start.11 = (bf16[2,384,16,32]{1,3,2,0:T(8,128)(2,1)}, bf16[2,384,16,32]{1,3,2,0:T(8,128)(2,1)S(1)}, u32[]{:S(2)}) copy-start(bf16[2,384,16,32]{1,3,2,0:T(8,128)(2,1)S(1)} %copy_dynamic-update-slice_fusion.3) | copy-start | bytes 2359300
  103.5 8.0 %copy-start.45 = (f32[256]{0:T(256)}, f32[256]{0:T(256)S(1)}, u32[]{:S(2)}) copy-start(f32[256]{0:T(256)S(1)} %get-tuple-element.62) | copy-start | bytes 3076
  113.4 7.6 %slice-start.2 = ((s8[6291456]{0:T(1024)(128)(4,1)}), s8[4194304]{0:T(1024)(128)(4,1)S(1)}, s32[]{:S(2)}) async-start(s8[6291456]{0:T(1024)(128)(4,1)} %bitcast.270), calls=%async_computation.2 | async-start | bytes 8388608
  116.1 4.9 %slice-start.3 = ((s8[6291456]{0:T(1024)(128)(4,1)}), s8[2097152]{0:T(1024)(128)(4,1)S(1)}, s32[]{:S(2)}) async-start(s8[6291456]{0:T(1024)(128)(4,1)} %bitcast.270), calls=%async_computation.3 | async-start | bytes 4194304
  124.1 3.1 %copy-start.22 = (bf16[2,128,16,32]{1,0,3,2:T(2,128)(2,1)S(1)}, bf16[2,128,16,32]{1,0,3,2:T(2,128)(2,1)}, u32[]{:S(2)}) copy-start(bf16[2,128,16,32]{1,0,3,2:T(2,128)(2,1)} %copy-done.21) | copy-start | bytes 786436
  147.2 12.1 %copy-start.14 = (f32[256,512]{1,0:T(8,128)S(1)}, f32[256,512]{1,0:T(8,128)}, u32[]{:S(2)}) copy-start(f32[256,512]{1,0:T(8,128)} %get-tuple-element.77) | copy-start | bytes 1572868
  153.2 7.4 %copy-start.35 = (bf16[512,512]{1,0:T(8,128)(2,1)}, bf16[512,512]{1,0:T(8,128)(2,1)S(1)}, u32[]{:S(2)}) copy-start(bf16[512,512]{1,0:T(8,128)(2,1)S(1)} %fusion.51) | copy-start | bytes 1572868
  154.1 42.3 %collective-permute-start.7 = (bf16[65920]{0:T(1024)(128)(2,1)}, bf16[65920]{0:T(1024)(128)(2,1)S(1)}, u32[]{:S(2)}, u32[]{:S(2)}) collective-permute-start(bf16[65920]{0:T(1024)(128)(2,1)} %pad_maximum_fusion.13), channel_id=1, source_target_pairs={{0,1},{1,2},{2,3},{3,4},{4,5},{5,6},{6,7},{7,8},{8,9},{9,10},{10,1... | collective-permute-start | bytes 395528 | tf_op jit(solution)/shard_map/ppermute | solution.py:27
  156.7 37.3 %collective-permute-start.6 = (bf16[65920]{0:T(1024)(128)(2,1)}, bf16[65920]{0:T(1024)(128)(2,1)S(1)}, u32[]{:S(2)}, u32[]{:S(2)}) collective-permute-start(bf16[65920]{0:T(1024)(128)(2,1)} %pad_maximum_fusion.12), channel_id=1, source_target_pairs={{1,0},{2,1},{3,2},{4,3},{5,4},{6,5},{7,6},{8,7},{9,8},{10,9},{11,1... | collective-permute-start | bytes 395528 | tf_op jit(solution)/shard_map/ppermute | solution.py:27
  193.9 12.7 %copy-start.19 = (bf16[65920]{0:T(1024)(128)(2,1)}, bf16[65920]{0:T(1024)(128)(2,1)S(1)}, u32[]{:S(2)}) copy-start(bf16[65920]{0:T(1024)(128)(2,1)S(1)} %collective-permute-done.6) | copy-start | bytes 395524
  196.4 10.2 %copy-start.17 = (bf16[65920]{0:T(1024)(128)(2,1)}, bf16[65920]{0:T(1024)(128)(2,1)S(1)}, u32[]{:S(2)}) copy-start(bf16[65920]{0:T(1024)(128)(2,1)S(1)} %collective-permute-done.7) | copy-start | bytes 395524
  198.8 7.8 %copy-start.51 = (f32[256]{0:T(256)S(1)}, f32[256]{0:T(256)}, u32[]{:S(2)}) copy-start(f32[256]{0:T(256)} %copy-done.50) | copy-start | bytes 3076
  198.8 7.8 %copy-start.41 = (f32[1,1,512]{2,1,0:T(1,128)S(1)}, f32[1,1,512]{2,1,0:T(1,128)}, u32[]{:S(2)}) copy-start(f32[1,1,512]{2,1,0:T(1,128)} %copy-done.40) | copy-start | bytes 6148
  198.8 7.8 %copy-start.47 = (f32[256]{0:T(256)S(1)}, f32[256]{0:T(256)}, u32[]{:S(2)}) copy-start(f32[256]{0:T(256)} %copy-done.46) | copy-start | bytes 3076
  198.8 7.8 %copy-start.49 = (f32[256]{0:T(256)S(1)}, f32[256]{0:T(256)}, u32[]{:S(2)}) copy-start(f32[256]{0:T(256)} %copy-done.48) | copy-start | bytes 3076
  206.6 4.8 %copy-start.36 = (f32[2,16,128]{2,1,0:T(8,128)S(1)}, f32[2,16,128]{2,1,0:T(8,128)}, u32[]{:S(2)}) copy-start(f32[2,16,128]{2,1,0:T(8,128)} %multiply_divide_fusion) | copy-start | bytes 49156
  210.7 5.8 %slice-start = ((s8[6291456]{0:T(1024)(128)(4,1)}), s8[4194304]{0:T(1024)(128)(4,1)S(1)}, s32[]{:S(2)}) async-start(s8[6291456]{0:T(1024)(128)(4,1)} %bitcast.268), calls=%async_computation | async-start | bytes 8388608
  211.4 5.2 %slice-start.1 = ((s8[6291456]{0:T(1024)(128)(4,1)}), s8[2097152]{0:T(1024)(128)(4,1)S(1)}, s32[]{:S(2)}) async-start(s8[6291456]{0:T(1024)(128)(4,1)} %bitcast.268), calls=%async_computation.1 | async-start | bytes 4194304
  211.4 5.2 %copy-start.32 = (f32[2,16,128]{2,1,0:T(8,128)S(1)}, f32[2,16,128]{2,1,0:T(8,128)}, u32[]{:S(2)}) copy-start(f32[2,16,128]{2,1,0:T(8,128)} %copy-done.31) | copy-start | bytes 49156
  211.4 5.2 %copy-start.43 = (pred[1,2,3,128]{3,1,2,0:T(4,128)(4,1)S(1)}, pred[1,2,3,128]{3,1,2,0:T(4,128)(4,1)}, u32[]{:S(2)}) copy-start(pred[1,2,3,128]{3,1,2,0:T(4,128)(4,1)} %copy-done.42) | copy-start | bytes 2308
  211.4 5.2 %copy-start.55 = (f32[16]{0:T(128)S(1)}, f32[16]{0:T(128)}, u32[]{:S(2)}) copy-start(f32[16]{0:T(128)} %copy-done.54) | copy-start | bytes 196
  219.0 3.3 %copy-start.34 = (f32[3,2,384]{2,1,0:T(2,128)S(1)}, f32[3,2,384]{2,1,0:T(2,128)}, u32[]{:S(2)}) copy-start(f32[3,2,384]{2,1,0:T(2,128)} %copy-done.33) | copy-start | bytes 27652
  219.0 3.3 %copy-start.38 = (f32[3,2,128]{2,1,0:T(2,128)S(1)}, f32[3,2,128]{2,1,0:T(2,128)}, u32[]{:S(2)}) copy-start(f32[3,2,128]{2,1,0:T(2,128)} %copy-done.37) | copy-start | bytes 9220
  219.0 3.7 %copy-start.20 = (bf16[65920]{0:T(1024)(128)(2,1)S(1)}, bf16[65920]{0:T(1024)(128)(2,1)}, u32[]{:S(2)}) copy-start(bf16[65920]{0:T(1024)(128)(2,1)} %copy-done.19) | copy-start | bytes 395524
  225.7 13.5 %copy-start.18 = (bf16[65920]{0:T(1024)(128)(2,1)S(1)}, bf16[65920]{0:T(1024)(128)(2,1)}, u32[]{:S(2)}) copy-start(bf16[65920]{0:T(1024)(128)(2,1)} %copy-done.17) | copy-start | bytes 395524
  225.7 15.9 %copy-start.1 = (bf16[128,512]{1,0:T(8,128)(2,1)S(1)}, bf16[128,512]{1,0:T(8,128)(2,1)}, u32[]{:S(2)}) copy-start(bf16[128,512]{1,0:T(8,128)(2,1)} %param.17) | copy-start | bytes 393220
  227.0 14.0 %copy-start.39 = (f32[1,3,4,128]{3,1,2,0:T(4,128)S(1)}, f32[1,3,4,128]{3,1,2,0:T(4,128)}, u32[]{:S(2)}) copy-start(f32[1,3,4,128]{3,1,2,0:T(4,128)} %copy.237) | copy-start | bytes 18436
  227.0 14.0 %copy-start.44 = (f32[3,2,128]{2,1,0:T(2,128)S(1)}, f32[3,2,128]{2,1,0:T(2,128)}, u32[]{:S(2)}) copy-start(f32[3,2,128]{2,1,0:T(2,128)} %get-tuple-element.6) | copy-start | bytes 9220
  232.8 6.6 %collective-permute-start.9 = (bf16[65920]{0:T(1024)(128)(2,1)S(1)}, bf16[65920]{0:T(1024)(128)(2,1)S(1)}, u32[]{:S(2)}, u32[]{:S(2)}) collective-permute-start(bf16[65920]{0:T(1024)(128)(2,1)S(1)} %pad_maximum_fusion.15), channel_id=1, source_target_pairs={{0,1},{1,2},{2,3},{3,4},{4,5},{5,6},{6,7},{7,8},{8,9},{9,10},{10,1... | collective-permute-start | bytes 395528 | tf_op jit(solution)/shard_map/ppermute | solution.py:27
  234.7 6.3 %collective-permute-start.8 = (bf16[65920]{0:T(1024)(128)(2,1)S(1)}, bf16[65920]{0:T(1024)(128)(2,1)S(1)}, u32[]{:S(2)}, u32[]{:S(2)}) collective-permute-start(bf16[65920]{0:T(1024)(128)(2,1)S(1)} %pad_maximum_fusion.14), channel_id=1, source_target_pairs={{1,0},{2,1},{3,2},{4,3},{5,4},{6,5},{7,6},{8,7},{9,8},{10,9},{11,1... | collective-permute-start | bytes 395528 | tf_op jit(solution)/shard_map/ppermute | solution.py:27
  (11 other events, 17.0 us)
where the time goes:
time: 244 us; the launch traced here: 242 us
  local copies, waits for them, and re-layouts  76.6 us (31%)
  matrix products  71.5 us (29%)
  blocking collectives  30.2 us (12%)
  starting transfers between devices  28.8 us (12%)
  other arithmetic  27 us (11%)
  waiting for transfers between devices  5.46 us (2%)
    psum x1, blocking collectives, local(): energy = lax.psum(local_total, 'chain').reshape(1)  30.2 us
    unnamed x160, local copies, waits for them, and re-layouts  26.6 us
    dot_general x6, matrix products, attend(): jnp.einsum('bhqk,bkhd->bqhd', probs, value_win, preferred_element_type=jn...  17 us
    slice x16, local copies, waits for them, and re-layouts, windows(): return jnp.concatenate([blocks[:-2], blocks[1:-1], blocks[2:]], axis=1)  13.5 us
    concatenate x18, local copies, waits for them, and re-layouts, windows(): return jnp.concatenate([blocks[:-2], blocks[1:-1], blocks[2:]], axis=1)  13.4 us
    ppermute x3, starting transfers between devices, padded(): lax.ppermute(lax.slice_in_dim(block, block.shape[dim] - width, None, axis...  11.8 us
    sub x2, matrix products, attend(): expo = jnp.exp(scores - peak)  11.2 us
    ppermute x4, starting transfers between devices, shifted(): lax.ppermute(value, axis, [(source, source + steps) for source in range(l...  11 us
  transfers between devices with their start and end apart: 10, of which 2 were waited for; matrix products, arithmetic and copies ran while one was open for 6% of the time, Pallas kernels for 0%

commit v1 on v0

v1 whole, which is shorter than its diff:
```python
import functools
import math

import jax
import jax.numpy as jnp
from jax import lax
from jax.experimental import pallas as pl
from jax.experimental.pallas import tpu as pltpu
from jax.sharding import PartitionSpec as P

MESH = pl.DeviceIdType.MESH
BLOCK = 128
LANES = 128
FAR = 1e30
EPS = 1e-06
GELU_A = math.sqrt(2.0 / math.pi)
GELU_B = 0.044715
F32 = jnp.float32
BF16 = jnp.bfloat16


def mm(a, b):
    return jnp.dot(a, b, preferred_element_type=F32)


def mm_nt(a, b):
    return lax.dot_general(a, b, (((1,), (1,)), ((), ())), preferred_element_type=F32)


def mm_tn(a, b):
    return lax.dot_general(a, b, (((0,), (0,)), ((), ())), preferred_element_type=F32)


def inv_rms(x):
    return lax.rsqrt(jnp.mean(x * x, axis=-1, keepdims=True) + EPS)


def rms_back(x, gain, dy):
    r = inv_rms(x)
    gy = gain * dy
    return r * gy - x * (r * r * r * jnp.mean(x * gy, axis=-1, keepdims=True))


def gelu(x):
    return 0.5 * x * (1.0 + jnp.tanh(GELU_A * (x + GELU_B * x * x * x)))


def gelu_slope(x):
    sq = x * x
    t = jnp.tanh(GELU_A * x * (1.0 + GELU_B * sq))
    return 0.5 * (1.0 + t) + (0.5 * GELU_A) * x * (1.0 - t * t) * (1.0 + 3.0 * GELU_B * sq)


def kernel(
    chain, nblk, layers, heads,
    spec_ref, pos_ref, blk_ref, gam_ref, gains_ref, og_ref, ro_ref, table_ref,
    wq_any, wk_any, wv_any, wo_any, wu_any, wd_any,
    e_ref, f_ref,
    wq, wk, wv, wo, wu, wd,
    sp_lo, sp_hi, ps_lo, ps_hi,
    xn, qs, ks, vs, kt, vt, probs, dist, gsum,
    att, xin, xmid, pre, dacc, dat, dqt, dks, dvs,
    gsend, grecv, fsend, frecv, fown, esend, erecv,
    wsem, ssem, rsem, essem, ersem,
):
    atoms = pos_ref.shape[1]
    width = table_ref.shape[1]
    nspec = table_ref.shape[0]
    hdim = width // heads
    per = LANES // hdim
    groups = width // LANES
    win = 3 * BLOCK
    ext = atoms + 2 * BLOCK
    own = slice(BLOCK, BLOCK + atoms)
    scale = hdim ** -0.5
    me = lax.axis_index("chain")
    has_l = me > 0
    has_r = me < chain - 1
    left = lax.rem(me + chain - 1, chain)
    right = lax.rem(me + 1, chain)
    steps = chain.bit_length() - 1

    loads = {}
    for layer in range(layers):
        for i, (src, dst) in enumerate(
            ((wk_any, wk), (wv_any, wv), (wq_any, wq), (wo_any, wo), (wu_any, wu), (wd_any, wd))
        ):
            copy = pltpu.make_async_copy(src.at[layer], dst.at[layer], wsem.at[layer, i])
            copy.start()
            loads[layer, i] = copy

    barrier = pltpu.get_barrier_semaphore()
    partners = []
    for s in range(steps):
        bit = 1 << s
        partners.append(me + bit - 2 * bit * lax.rem(lax.div(me, bit), 2))

    def greet(to):
        pl.semaphore_signal(barrier, inc=1, device_id={"chain": to}, device_id_type=MESH)

    for partner in partners[1:]:
        greet(partner)

    @pl.when(has_l)
    def _():
        greet(left)

    @pl.when(has_r)
    def _():
        greet(right)

    pl.semaphore_wait(
        barrier, max(0, steps - 1) + has_l.astype(jnp.int32) + has_r.astype(jnp.int32)
    )

    def swap(slot, first, last, high, low):
        to_left = pltpu.make_async_remote_copy(
            src_ref=first, dst_ref=high, send_sem=ssem.at[slot, 0], recv_sem=rsem.at[slot, 0],
            device_id={"chain": left}, device_id_type=MESH,
        )
        to_right = pltpu.make_async_remote_copy(
            src_ref=last, dst_ref=low, send_sem=ssem.at[slot, 1], recv_sem=rsem.at[slot, 1],
            device_id={"chain": right}, device_id_type=MESH,
        )
        return to_left, to_right

    def start(pair):
        pl.when(has_l)(pair[0].start)
        pl.when(has_r)(pair[1].start)

    def received(pair):
        pl.when(has_r)(pair[0].wait_recv)
        pl.when(has_l)(pair[1].wait_recv)

    def sent(pair):
        pl.when(has_l)(pair[0].wait_send)
        pl.when(has_r)(pair[1].wait_send)

    head_first = pl.ds(0, BLOCK)
    head_last = pl.ds(atoms - BLOCK, BLOCK)
    swap_sp = swap(0, spec_ref.at[:, head_first], spec_ref.at[:, head_last], sp_hi, sp_lo)
    swap_ps = swap(1, pos_ref.at[:, head_first], pos_ref.at[:, head_last], ps_hi, ps_lo)
    start(swap_sp)
    start(swap_ps)
    swap_xn = swap(
        2,
        xn.at[1, pl.ds(BLOCK, BLOCK)], xn.at[1, pl.ds(atoms, BLOCK)],
        xn.at[1, pl.ds(BLOCK + atoms, BLOCK)], xn.at[1, pl.ds(0, BLOCK)],
    )
    swap_g = swap(3, gsend.at[0], gsend.at[1], grecv.at[1], grecv.at[0])
    swap_f = swap(4, fsend.at[0], fsend.at[1], frecv.at[1], frecv.at[0])

    @pl.when(me == 0)
    def _():
        sp_lo[...] = jnp.zeros_like(sp_lo)
        ps_lo[...] = jnp.zeros_like(ps_lo)
        xn[1, 0:BLOCK, :] = jnp.zeros((BLOCK, width), BF16)
        grecv[0] = jnp.zeros((BLOCK, width), BF16)
        frecv[0] = jnp.zeros((8, BLOCK), F32)

    @pl.when(me == chain - 1)
    def _():
        sp_hi[...] = jnp.zeros_like(sp_hi)
        ps_hi[...] = jnp.zeros_like(ps_hi)
        xn[1, BLOCK + atoms : ext, :] = jnp.zeros((BLOCK, width), BF16)
        grecv[1] = jnp.zeros((BLOCK, width), BF16)
        frecv[1] = jnp.zeros((8, BLOCK), F32)

    table = table_ref[...]

    def embed(row):
        count = row.shape[1]
        hot = (lax.broadcasted_iota(jnp.int32, (nspec, count), 0) == row).astype(F32).astype(BF16)
        return mm_tn(hot, table)

    def norm(x, gain):
        return (x * inv_rms(x) * gain).astype(BF16)

    gain_a = [gains_ref[layer, 0:1, :] for layer in range(layers)]
    gain_b = [gains_ref[layer, 1:2, :] for layer in range(layers)]

    state = embed(spec_ref[...])
    xn[0, own, :] = norm(state, gain_a[0])
    received(swap_sp)
    xn[0, 0:BLOCK, :] = norm(embed(sp_lo[...]), gain_a[0])
    xn[0, BLOCK + atoms : ext, :] = norm(embed(sp_hi[...]), gain_a[0])
    received(swap_ps)

    rows = [ps_lo] + [pos_ref.at[:, pl.ds(b * BLOCK, BLOCK)] for b in range(nblk)] + [ps_hi]
    columns = [
        [jnp.transpose(jnp.broadcast_to(ref[c : c + 1, :], (BLOCK, BLOCK))) for c in range(3)]
        for ref in rows
    ]
    for b in range(nblk):
        for s in range(3):
            total = None
            for c in range(3):
                diff = columns[b + s][c] - rows[b + 1][c : c + 1, :]
                total = diff * diff if total is None else total + diff * diff
            block = blk_ref[b, s]
            listed = jnp.logical_and(block == me * nblk + (b - 1 + s), block >= 0)
            dist[b, s * BLOCK : (s + 1) * BLOCK, :] = jnp.where(listed, total, FAR)

    lane = lax.broadcasted_iota(jnp.int32, (1, LANES), 1)
    masks = [
        jnp.logical_and(lane >= i * hdim, lane < (i + 1) * hdim).astype(F32).astype(BF16)
        for i in range(per)
    ]
    gsum[...] = jnp.zeros_like(gsum)

    def keys_values(layer, part):
        src = xn[layer, part, :]
        k = mm(src, wk[layer])
        v = mm(src, wv[layer])
        ks[layer, part, :] = k.astype(BF16)
        vs[layer, part, :] = v.astype(BF16)
        vt[:, part] = jnp.transpose(v).astype(BF16)
        if layer:
            kt[:, part] = jnp.transpose(k).astype(BF16)

    def attend(layer):
        def body(g, carry):
            lanes = pl.ds(pl.multiple_of(g * LANES, LANES), LANES)
            for b in range(nblk):
                key = ks[layer, b * BLOCK : b * BLOCK + win, lanes]
                query = qs[layer, b * BLOCK : (b + 1) * BLOCK, lanes]
                far = dist[b]
                for i in range(per):
                    h = g * per + i
                    score = mm_nt(key, query * masks[i]) - (gam_ref[layer, h] / scale) * far
                    peak = jnp.max(score, axis=0, keepdims=True)
                    expo = jnp.exp2((score - peak) * (scale * math.log2(math.e)))
                    inv = 1.0 / jnp.sum(expo, axis=0, keepdims=True)
                    p = (expo * inv).astype(BF16)
                    probs[layer, h, b] = p
                    part = pl.ds(pl.multiple_of(h * hdim, hdim), hdim)
                    att[layer, part, b * BLOCK : (b + 1) * BLOCK] = mm(
                        vt[part, b * BLOCK : b * BLOCK + win], p
                    )
            return carry

        lax.fori_loop(0, groups, body, 0)

    for layer in range(layers):
        xin[layer] = state
        if layer == 0:
            loads[layer, 0].wait()
            loads[layer, 1].wait()
            keys_values(layer, slice(0, ext))
            loads[layer, 2].wait()
            qs[layer] = mm(xn[layer, own, :], wq[layer]).astype(BF16)
        else:
            xn[layer, own, :] = norm(state, gain_a[layer])
            loads[layer, 0].wait()
            loads[layer, 1].wait()
            loads[layer, 2].wait()
            start(swap_xn)
            qs[layer] = mm(xn[layer, own, :], wq[layer]).astype(BF16)
            keys_values(layer, own)
            received(swap_xn)
            keys_values(layer, slice(0, BLOCK))
            keys_values(layer, slice(BLOCK + atoms, ext))
        attend(layer)
        loads[layer, 3].wait()
        mid = state + mm(jnp.transpose(att[layer]).astype(BF16), wo[layer])
        xmid[layer] = mid
        loads[layer, 4].wait()
        hidden = mm(norm(mid, gain_b[layer]), wu[layer])
        pre[layer] = hidden
        loads[layer, 5].wait()
        state = mid + mm(gelu(hidden).astype(BF16), wd[layer])

    r = inv_rms(state)
    gy = og_ref[...] * ro_ref[...]
    energy = jnp.sum(state * r * gy)
    grad = r * gy - state * (r * r * r * jnp.mean(state * gy, axis=-1, keepdims=True))

    ecopies = [
        pltpu.make_async_remote_copy(
            src_ref=esend.at[s], dst_ref=erecv.at[s], send_sem=essem.at[s], recv_sem=ersem.at[s],
            device_id={"chain": partners[s]}, device_id_type=MESH,
        )
        for s in range(steps)
    ]
    esend[0] = jnp.broadcast_to(energy, (8, LANES))
    done = [0]

    def advance(last=False):
        s = done[0]
        if s > 0 and s <= steps:
            ecopies[s - 1].wait_recv()
            esend[s] = esend[s - 1] + erecv[s - 1]
        if s < steps:
            ecopies[s].start()
        done[0] = s + 1

    def slopes(layer, grad):
        du = mm_nt(grad.astype(BF16), wd[layer]).astype(BF16).astype(F32)
        dpre = (du * gelu_slope(pre[layer])).astype(BF16)
        dm = mm_nt(dpre, wu[layer]).astype(BF16).astype(F32)
        grad = grad + rms_back(xmid[layer], gain_b[layer], dm)
        da = mm_nt(grad.astype(BF16), wo[layer])
        dacc[...] = da.astype(BF16)
        dat[...] = jnp.transpose(da)
        return grad

    def attend_back(layer):
        deep = layer > 0

        def body(g, carry):
            lanes = pl.ds(pl.multiple_of(g * LANES, LANES), LANES)
            if deep:
                dks[:, lanes] = jnp.zeros((ext, LANES), F32)
                dvs[:, lanes] = jnp.zeros((ext, LANES), F32)
            for b in range(nblk):
                rows_b = slice(b * BLOCK, (b + 1) * BLOCK)
                window = slice(b * BLOCK, b * BLOCK + win)
                value = vs[layer, window, lanes]
                da = dacc[rows_b, lanes]
                pieces = []
                total = gsum[b]
                for i in range(per):
                    h = g * per + i
                    part = pl.ds(pl.multiple_of(h * hdim, hdim), hdim)
                    delta = jnp.sum(
                        dat[part, rows_b] * att[layer, part, rows_b], axis=0, keepdims=True
                    )
                    dp = mm_nt(value, da * masks[i])
                    ds = probs[layer, h, b].astype(F32) * (dp - delta)
                    total = total - gam_ref[layer, h] * ds
                    if deep:
                        dsb = ds.astype(BF16)
                        dqt[part, rows_b] = mm(kt[part, window], dsb)
                        pieces.append(dsb)
                gsum[b] = total
                if deep:
                    query = qs[layer, rows_b, lanes]
                    dks[window, lanes] += mm(
                        jnp.concatenate(pieces, axis=1),
                        jnp.concatenate([query * m for m in masks], axis=0),
                    )
                    dvs[window, lanes] += mm(
                        jnp.concatenate([probs[layer, g * per + i, b] for i in range(per)], axis=1),
                        jnp.concatenate([da * m for m in masks], axis=0),
                    )
            return carry

        lax.fori_loop(0, groups, body, 0)

    for layer in reversed(range(layers)):
        if layer == layers - 1:
            advance()
        grad = slopes(layer, grad)
        advance()
        attend_back(layer)
        if layer:
            def into(part):
                return mm_nt((dks[part, :] * scale).astype(BF16), wk[layer]) + mm_nt(
                    dvs[part, :].astype(BF16), wv[layer]
                )

            gsend[0] = into(slice(0, BLOCK)).astype(BF16)
            gsend[1] = into(slice(BLOCK + atoms, ext)).astype(BF16)
            dq = (jnp.transpose(dqt[...]) * scale).astype(BF16)
            start(swap_g)
            dn = into(own) + mm_nt(dq, wq[layer])
            advance()
            received(swap_g)
            head = [grecv[0].astype(F32)] + [None] * (nblk - 1)
            dn_blocks = []
            for b in range(nblk):
                piece = dn[b * BLOCK : (b + 1) * BLOCK]
                if b == 0:
                    piece = piece + grecv[0].astype(F32)
                if b == nblk - 1:
                    piece = piece + grecv[1].astype(F32)
                dn_blocks.append(piece)
            dn = jnp.concatenate(dn_blocks, axis=0).astype(BF16).astype(F32)
            grad = grad + rms_back(xin[layer], gain_a[layer], dn)

    def rows8(ref):
        return jnp.concatenate(
            [ref[...], jnp.ones((1, BLOCK), F32), jnp.zeros((4, BLOCK), F32)], axis=0
        )

    full = [rows8(ref) for ref in rows]
    parts = [jnp.zeros((8, BLOCK), F32) for _ in rows]
    exact = lax.Precision.HIGHEST
    for b in range(nblk):
        fq = full[b + 1]
        for s in range(3):
            j = b + s
            g = gsum[b, s * BLOCK : (s + 1) * BLOCK, :]
            to_q = jnp.dot(full[j], g, precision=exact, preferred_element_type=F32)
            to_k = lax.dot_general(
                fq, g, (((1,), (1,)), ((), ())), precision=exact, preferred_element_type=F32
            )
            parts[b + 1] = parts[b + 1] + 2.0 * (fq * to_q[3:4, :] - to_q)
            parts[j] = parts[j] + 2.0 * (full[j] * to_k[3:4, :] - to_k)
    fsend[0] = parts[0]
    fsend[1] = parts[nblk + 1]
    for b in range(nblk):
        fown[:, b * BLOCK : (b + 1) * BLOCK] = parts[b + 1]
    start(swap_f)
    while done[0] <= steps:
        advance()
    for s in range(steps):
        ecopies[s].wait_send()
    e_ref[0] = jnp.max(esend[steps])
    sent(swap_sp)
    sent(swap_ps)
    sent(swap_xn)
    sent(swap_g)
    received(swap_f)
    fown[:, 0:BLOCK] += frecv[0]
    fown[:, atoms - BLOCK : atoms] += frecv[1]
    f_ref[...] = -fown[0:3, :]
    sent(swap_f)


def solution(mesh):
    chain = mesh.shape["chain"]

    def local(
        species, positions, block_list, embed_table, w_query, w_key, w_value, w_out, w_up, w_down,
        norm_gains, gammas, out_gain, readout,
    ):
        atoms = species.shape[0]
        nblk = atoms // BLOCK
        width = embed_table.shape[1]
        layers, heads = gammas.shape
        ff = w_up.shape[2]
        ext = atoms + 2 * BLOCK
        win = 3 * BLOCK
        steps = chain.bit_length() - 1
        if layers != 2 or chain != 1 << steps:
            raise ValueError("unsupported sizes")
        vmem = pl.BlockSpec(memory_space=pltpu.VMEM)
        smem = pl.BlockSpec(memory_space=pltpu.SMEM)
        anys = pl.BlockSpec(memory_space=pl.ANY)
        V = pltpu.VMEM
        energy, forces = pl.pallas_call(
            functools.partial(kernel, chain, nblk, layers, heads),
            out_shape=(
                jax.ShapeDtypeStruct((1,), F32),
                jax.ShapeDtypeStruct((3, atoms), F32),
            ),
            in_specs=[vmem, vmem, smem, smem, vmem, vmem, vmem, vmem] + [anys] * 6,
            out_specs=(smem, vmem),
            scratch_shapes=[
                V((layers, width, width), BF16), V((layers, width, width), BF16),
                V((layers, width, width), BF16), V((layers, width, width), BF16),
                V((layers, width, ff), BF16), V((layers, ff, width), BF16),
                V((1, BLOCK), jnp.int32), V((1, BLOCK), jnp.int32),
                V((3, BLOCK), F32), V((3, BLOCK), F32),
                V((layers, ext, width), BF16),
                V((layers, atoms, width), BF16),
                V((layers, ext, width), BF16), V((layers, ext, width), BF16),
                V((width, ext), BF16), V((width, ext), BF16),
                V((layers, heads, nblk, win, BLOCK), BF16),
                V((nblk, win, BLOCK), F32), V((nblk, win, BLOCK), F32),
                V((layers, width, atoms), F32),
                V((layers, atoms, width), F32), V((layers, atoms, width), F32),
                V((layers, atoms, ff), F32),
                V((atoms, width), BF16), V((width, atoms), F32),
                V((width, atoms), F32), V((ext, width), F32), V((ext, width), F32),
                V((2, BLOCK, width), BF16), V((2, BLOCK, width), BF16),
                V((2, 8, BLOCK), F32), V((2, 8, BLOCK), F32), V((8, atoms), F32),
                V((steps + 1, 8, LANES), F32), V((steps + 1, 8, LANES), F32),
                pltpu.SemaphoreType.DMA((layers, 6)),
                pltpu.SemaphoreType.DMA((5, 2)), pltpu.SemaphoreType.DMA((5, 2)),
                pltpu.SemaphoreType.DMA((steps + 1,)), pltpu.SemaphoreType.DMA((steps + 1,)),
            ],
            compiler_params=pltpu.CompilerParams(
                collective_id=0, has_side_effects=True, vmem_limit_bytes=60 * 1024 * 1024
            ),
        )(
            species.reshape(1, atoms), positions, block_list, gammas, norm_gains,
            out_gain.reshape(1, width), readout.reshape(1, width), embed_table,
            w_query, w_key, w_value, w_out, w_up, w_down,
        )
        return energy, forces

    shard = P(("frames", "chain"))
    return jax.shard_map(
        local,
        mesh=mesh,
        in_specs=(shard, P(None, ("frames", "chain")), P(("frames", "chain"), None)) + (P(),) * 11,
        out_specs=(P("frames"), P(None, ("frames", "chain"))),
        check_vma=False,
    )
```

time: 244 us -> 56.2 us (0.23)
  local copies, waits for them, and re-layouts: 76.6 us -> 1.27 us
  matrix products: 71.5 us -> 0 us
  Pallas kernels: 0 us -> 51.5 us
  blocking collectives: 30.2 us -> 0 us
  starting transfers between devices: 28.8 us -> 0 us
  other arithmetic: 27 us -> 0 us
  waiting for transfers between devices: 5.46 us -> 0 us
    dot_general x32 -> x0, matrix products: 60.2 us -> none  [the longest x6 17 us: attend(): jnp.einsum('bhqk,bkhd->bqhd', probs, value_win, preferred_element_type=jn...]
    pallas_call x0 -> x1, Pallas kernels: none -> 51.5 us  [local(): pl.pallas_call(functools.partial(kernel, chain, nblk, layers, heads), out...]
    psum x1 -> x0, blocking collectives: 30.2 us -> none  [local(): energy = lax.psum(local_total, 'chain').reshape(1)]
    ppermute x10 -> x0, starting transfers between devices: 28.8 us -> none  [the longest x3 11.8 us: padded(): lax.ppermute(lax.slice_in_dim(block, block.shape[dim] - width, None, axis...]
    unnamed x160 -> x1, local copies, waits for them, and re-layouts: 26.6 us -> 1.27 us
    slice x27 -> x0, local copies, waits for them, and re-layouts: 17.3 us -> none  [the longest x16 13.5 us: windows(): return jnp.concatenate([blocks[:-2], blocks[1:-1], blocks[2:]], axis=1)]
    concatenate x18 -> x0, local copies, waits for them, and re-layouts: 13.4 us -> none  [windows(): return jnp.concatenate([blocks[:-2], blocks[1:-1], blocks[2:]], axis=1)]
    sub x2 -> x0, matrix products: 11.2 us -> none  [attend(): expo = jnp.exp(scores - peak)]
  transfers between devices with their start and end apart: 10 -> 0, of which waited for: 2 -> 0; matrix products, arithmetic and copies ran while one was open for 6% -> 0% of each run, Pallas kernels for 0% -> 0%
where the time goes in v1:
time: 56.2 us; the launch traced here: 55.2 us
  Pallas kernels  51.5 us (92%)
  between operations  2.41 us (4%)
  local copies, waits for them, and re-layouts  1.27 us (2%)
    pallas_call x1, Pallas kernels, local(): pl.pallas_call(functools.partial(kernel, chain, nblk, layers, heads), out...  51.5 us
    unnamed x1, local copies, waits for them, and re-layouts  1.27 us

profile of v1, /device:TPU:1, one launch (start us, length us, event | category | flops | bytes accessed | tf_op | source)
XLA Modules:
  0.0 55.2 jit_solution(2077103679940008805)
XLA Ops:
  0.6 51.5 %shard_map.149 = (f32[1]{0:T(128)}, f32[3,256]{1,0:T(4,128)}) custom-call(s32[1,256]{1,0:T(1,128)} %bitcast.5, f32[3,256]{1,0:T(4,128)} %pos_ref.1, s32[2,3]{1,0:T(2,128)} %blk_ref.1, f32[2,16]{1,0:T(2,128)} %gam_ref.1, f32[2,2,512]{2,1,0:T(2,128)} %gains_ref.1, f32[1,512]{1,0:T(1,128)} %bitcast.3, f32[1,512]{1,0:T(1,128)} %bitcast.4, ...), custom_call_target="tpu_custom_call" | custom-call | tf_op jit(solution)/shard_map/pallas_call | solution.py:442
  52.8 1.3 %copy.19 = f32[3,256]{1,0:T(4,128)} copy(f32[3,256]{1,0:T(4,128)} %get-tuple-element.5) | data formatting | bytes 6144

commit v2 on v1

--- a/solution.py
+++ b/solution.py
@@ -41,14 +41,11 @@
     return r * gy - x * (r * r * r * jnp.mean(x * gy, axis=-1, keepdims=True))
 
 
-def gelu(x):
-    return 0.5 * x * (1.0 + jnp.tanh(GELU_A * (x + GELU_B * x * x * x)))
-
-
-def gelu_slope(x):
+def gelu_and_slope(x):
     sq = x * x
-    t = jnp.tanh(GELU_A * x * (1.0 + GELU_B * sq))
-    return 0.5 * (1.0 + t) + (0.5 * GELU_A) * x * (1.0 - t * t) * (1.0 + 3.0 * GELU_B * sq)
+    h = 0.5 + 0.5 * jnp.tanh(x * (GELU_A + (GELU_A * GELU_B) * sq))
+    u = x * h
+    return u, h + u * (1.0 - h) * (2.0 * GELU_A + (6.0 * GELU_A * GELU_B) * sq)
 
 
 def kernel(
@@ -60,7 +57,7 @@
     sp_lo, sp_hi, ps_lo, ps_hi,
     xn, qs, ks, vs, kt, vt, probs, dist, gsum,
     att, xin, xmid, pre, dacc, dat, dqt, dks, dvs,
-    gsend, grecv, fsend, frecv, fown, esend, erecv,
+    gsend, grecv, fsend, frecv, fown, esend, erecv, scores, dsc, invs,
     wsem, ssem, rsem, essem, ersem,
 ):
     atoms = pos_ref.shape[1]
@@ -73,6 +70,7 @@
     ext = atoms + 2 * BLOCK
     own = slice(BLOCK, BLOCK + atoms)
     scale = hdim ** -0.5
+    qscale = scale * math.log2(math.e)
     me = lax.axis_index("chain")
     has_l = me > 0
     has_r = me < chain - 1
@@ -218,25 +216,31 @@
         if layer:
             kt[:, part] = jnp.transpose(k).astype(BF16)
 
+    units = [(b, i) for b in range(nblk) for i in range(per)]
+    ones = jnp.ones((16, win), BF16)
+
     def attend(layer):
         def body(g, carry):
             lanes = pl.ds(pl.multiple_of(g * LANES, LANES), LANES)
-            for b in range(nblk):
+            peaks = []
+            for u, (b, i) in enumerate(units):
                 key = ks[layer, b * BLOCK : b * BLOCK + win, lanes]
                 query = qs[layer, b * BLOCK : (b + 1) * BLOCK, lanes]
-                far = dist[b]
-                for i in range(per):
-                    h = g * per + i
-                    score = mm_nt(key, query * masks[i]) - (gam_ref[layer, h] / scale) * far
-                    peak = jnp.max(score, axis=0, keepdims=True)
-                    expo = jnp.exp2((score - peak) * (scale * math.log2(math.e)))
-                    inv = 1.0 / jnp.sum(expo, axis=0, keepdims=True)
-                    p = (expo * inv).astype(BF16)
-                    probs[layer, h, b] = p
-                    part = pl.ds(pl.multiple_of(h * hdim, hdim), hdim)
-                    att[layer, part, b * BLOCK : (b + 1) * BLOCK] = mm(
-                        vt[part, b * BLOCK : b * BLOCK + win], p
-                    )
+                slope = gam_ref[layer, g * per + i] * math.log2(math.e)
+                score = mm_nt(key, query * masks[i]) - slope * dist[b]
+                scores[u] = score
+                peaks.append(jnp.max(score, axis=0, keepdims=True))
+            for u, (b, i) in enumerate(units):
+                probs[layer, g * per + i, b] = jnp.exp2(scores[u] - peaks[u]).astype(BF16)
+            for u, (b, i) in enumerate(units):
+                h = g * per + i
+                part = pl.ds(pl.multiple_of(h * hdim, hdim), hdim)
+                cols = slice(b * BLOCK, (b + 1) * BLOCK)
+                value = jnp.concatenate([vt[part, b * BLOCK : b * BLOCK + win], ones], axis=0)
+                mixed = mm(value, probs[layer, h, b])
+                inv = 1.0 / mixed[hdim : hdim + 1, :]
+                invs[layer, h, :, cols] = inv
+                att[layer, part, cols] = mixed[0:hdim, :] * inv
             return carry
 
         lax.fori_loop(0, groups, body, 0)
@@ -248,14 +252,14 @@
             loads[layer, 1].wait()
             keys_values(layer, slice(0, ext))
             loads[layer, 2].wait()
-            qs[layer] = mm(xn[layer, own, :], wq[layer]).astype(BF16)
+            qs[layer] = (mm(xn[layer, own, :], wq[layer]) * qscale).astype(BF16)
         else:
             xn[layer, own, :] = norm(state, gain_a[layer])
             loads[layer, 0].wait()
             loads[layer, 1].wait()
             loads[layer, 2].wait()
             start(swap_xn)
-            qs[layer] = mm(xn[layer, own, :], wq[layer]).astype(BF16)
+            qs[layer] = (mm(xn[layer, own, :], wq[layer]) * qscale).astype(BF16)
             keys_values(layer, own)
             received(swap_xn)
             keys_values(layer, slice(0, BLOCK))
@@ -266,9 +270,9 @@
         xmid[layer] = mid
         loads[layer, 4].wait()
         hidden = mm(norm(mid, gain_b[layer]), wu[layer])
-        pre[layer] = hidden
+        hidden, pre[layer] = gelu_and_slope(hidden)
         loads[layer, 5].wait()
-        state = mid + mm(gelu(hidden).astype(BF16), wd[layer])
+        state = mid + mm(hidden.astype(BF16), wd[layer])
 
     r = inv_rms(state)
     gy = og_ref[...] * ro_ref[...]
@@ -296,12 +300,15 @@
 
     def slopes(layer, grad):
         du = mm_nt(grad.astype(BF16), wd[layer]).astype(BF16).astype(F32)
-        dpre = (du * gelu_slope(pre[layer])).astype(BF16)
+        dpre = (du * pre[layer]).astype(BF16)
         dm = mm_nt(dpre, wu[layer]).astype(BF16).astype(F32)
         grad = grad + rms_back(xmid[layer], gain_b[layer], dm)
         da = mm_nt(grad.astype(BF16), wo[layer])
-        dacc[...] = da.astype(BF16)
-        dat[...] = jnp.transpose(da)
+        da = jnp.transpose(da)
+        for h in range(heads):
+            part = slice(h * hdim, (h + 1) * hdim)
+            dat[part, :] = da[part, :] * invs[layer, h]
+        dacc[...] = jnp.transpose(dat[...]).astype(BF16)
         return grad
 
     def attend_back(layer):
@@ -317,7 +324,6 @@
                 window = slice(b * BLOCK, b * BLOCK + win)
                 value = vs[layer, window, lanes]
                 da = dacc[rows_b, lanes]
-                pieces = []
                 total = gsum[b]
                 for i in range(per):
                     h = g * per + i
@@ -329,20 +335,26 @@
                     ds = probs[layer, h, b].astype(F32) * (dp - delta)
                     total = total - gam_ref[layer, h] * ds
                     if deep:
-                        dsb = ds.astype(BF16)
-                        dqt[part, rows_b] = mm(kt[part, window], dsb)
-                        pieces.append(dsb)
+                        dsc[b, :, i * BLOCK : (i + 1) * BLOCK] = ds.astype(BF16)
                 gsum[b] = total
-                if deep:
+            if deep:
+                for b in range(nblk):
+                    rows_b = slice(b * BLOCK, (b + 1) * BLOCK)
+                    window = slice(b * BLOCK, b * BLOCK + win)
                     query = qs[layer, rows_b, lanes]
+                    da = dacc[rows_b, lanes]
                     dks[window, lanes] += mm(
-                        jnp.concatenate(pieces, axis=1),
-                        jnp.concatenate([query * m for m in masks], axis=0),
+                        dsc[b], jnp.concatenate([query * m for m in masks], axis=0)
                     )
                     dvs[window, lanes] += mm(
                         jnp.concatenate([probs[layer, g * per + i, b] for i in range(per)], axis=1),
                         jnp.concatenate([da * m for m in masks], axis=0),
                     )
+                    for i in range(per):
+                        part = pl.ds(pl.multiple_of((g * per + i) * hdim, hdim), hdim)
+                        dqt[part, rows_b] = mm(
+                            kt[part, window], dsc[b, :, i * BLOCK : (i + 1) * BLOCK]
+                        )
             return carry
 
         lax.fori_loop(0, groups, body, 0)
@@ -355,7 +367,7 @@
         attend_back(layer)
         if layer:
             def into(part):
-                return mm_nt((dks[part, :] * scale).astype(BF16), wk[layer]) + mm_nt(
+                return mm_nt((dks[part, :] * math.log(2.0)).astype(BF16), wk[layer]) + mm_nt(
                     dvs[part, :].astype(BF16), wv[layer]
                 )
 
@@ -366,7 +378,6 @@
             dn = into(own) + mm_nt(dq, wq[layer])
             advance()
             received(swap_g)
-            head = [grecv[0].astype(F32)] + [None] * (nblk - 1)
             dn_blocks = []
             for b in range(nblk):
                 piece = dn[b * BLOCK : (b + 1) * BLOCK]
@@ -467,6 +478,9 @@
                 V((2, BLOCK, width), BF16), V((2, BLOCK, width), BF16),
                 V((2, 8, BLOCK), F32), V((2, 8, BLOCK), F32), V((8, atoms), F32),
                 V((steps + 1, 8, LANES), F32), V((steps + 1, 8, LANES), F32),
+                V((nblk * (LANES * heads // width), win, BLOCK), F32),
+                V((nblk, win, LANES * heads // width * BLOCK), BF16),
+                V((layers, heads, 1, atoms), F32),
                 pltpu.SemaphoreType.DMA((layers, 6)),
                 pltpu.SemaphoreType.DMA((5, 2)), pltpu.SemaphoreType.DMA((5, 2)),
                 pltpu.SemaphoreType.DMA((steps + 1,)), pltpu.SemaphoreType.DMA((steps + 1,)),

time: 56.2 us -> 45.9 us (0.82)
  Pallas kernels: 51.5 us -> 41.5 us
    pallas_call x1, Pallas kernels: 51.5 us -> 41.5 us  [local(): pl.pallas_call(functools.partial(kernel, chain, nblk, layers, heads), out...]
where the time goes in v2:
time: 45.9 us; the launch traced here: 45.2 us
  Pallas kernels  41.5 us (90%)
  between operations  2.41 us (5%)
  local copies, waits for them, and re-layouts  1.27 us (3%)
    pallas_call x1, Pallas kernels, local(): pl.pallas_call(functools.partial(kernel, chain, nblk, layers, heads), out...  41.5 us
    unnamed x1, local copies, waits for them, and re-layouts  1.27 us

profile of v2, /device:TPU:1, one launch (start us, length us, event | category | flops | bytes accessed | tf_op | source)
XLA Modules:
  0.0 45.2 jit_solution(13142906507806132612)
XLA Ops:
  0.6 41.5 %shard_map.149 = (f32[1]{0:T(128)}, f32[3,256]{1,0:T(4,128)}) custom-call(s32[1,256]{1,0:T(1,128)} %bitcast.5, f32[3,256]{1,0:T(4,128)} %pos_ref.1, s32[2,3]{1,0:T(2,128)} %blk_ref.1, f32[2,16]{1,0:T(2,128)} %gam_ref.1, f32[2,2,512]{2,1,0:T(2,128)} %gains_ref.1, f32[1,512]{1,0:T(1,128)} %bitcast.3, f32[1,512]{1,0:T(1,128)} %bitcast.4, ...), custom_call_target="tpu_custom_call" | custom-call | tf_op jit(solution)/shard_map/pallas_call | solution.py:453
  42.8 1.3 %copy.19 = f32[3,256]{1,0:T(4,128)} copy(f32[3,256]{1,0:T(4,128)} %get-tuple-element.5) | data formatting | bytes 6144

commit v3 on v2

--- a/solution.py
+++ b/solution.py
@@ -227,7 +227,7 @@
                 key = ks[layer, b * BLOCK : b * BLOCK + win, lanes]
                 query = qs[layer, b * BLOCK : (b + 1) * BLOCK, lanes]
                 slope = gam_ref[layer, g * per + i] * math.log2(math.e)
-                score = mm_nt(key, query * masks[i]) - slope * dist[b]
+                score = mm_nt(key, query * masks[i]) * qscale - slope * dist[b]
                 scores[u] = score
                 peaks.append(jnp.max(score, axis=0, keepdims=True))
             for u, (b, i) in enumerate(units):
@@ -252,14 +252,14 @@
             loads[layer, 1].wait()
             keys_values(layer, slice(0, ext))
             loads[layer, 2].wait()
-            qs[layer] = (mm(xn[layer, own, :], wq[layer]) * qscale).astype(BF16)
+            qs[layer] = mm(xn[layer, own, :], wq[layer]).astype(BF16)
         else:
             xn[layer, own, :] = norm(state, gain_a[layer])
             loads[layer, 0].wait()
             loads[layer, 1].wait()
             loads[layer, 2].wait()
             start(swap_xn)
-            qs[layer] = (mm(xn[layer, own, :], wq[layer]) * qscale).astype(BF16)
+            qs[layer] = mm(xn[layer, own, :], wq[layer]).astype(BF16)
             keys_values(layer, own)
             received(swap_xn)
             keys_values(layer, slice(0, BLOCK))
@@ -367,7 +367,7 @@
         attend_back(layer)
         if layer:
             def into(part):
-                return mm_nt((dks[part, :] * math.log(2.0)).astype(BF16), wk[layer]) + mm_nt(
+                return mm_nt((dks[part, :] * scale).astype(BF16), wk[layer]) + mm_nt(
                     dvs[part, :].astype(BF16), wv[layer]
                 )
 

time: 45.9 us -> 46.2 us (level)
  no operation moved by 1% of the time
where the time goes in v3:
time: 46.2 us; the launch traced here: 45.4 us
  Pallas kernels  41.8 us (90%)
  between operations  2.41 us (5%)
  local copies, waits for them, and re-layouts  1.27 us (3%)
    pallas_call x1, Pallas kernels, local(): pl.pallas_call(functools.partial(kernel, chain, nblk, layers, heads), out...  41.8 us
    unnamed x1, local copies, waits for them, and re-layouts  1.27 us

profile of v3, /device:TPU:1, one launch (start us, length us, event | category | flops | bytes accessed | tf_op | source)
XLA Modules:
  0.0 45.4 jit_solution(8897633160345449369)
XLA Ops:
  0.6 41.8 %shard_map.149 = (f32[1]{0:T(128)}, f32[3,256]{1,0:T(4,128)}) custom-call(s32[1,256]{1,0:T(1,128)} %bitcast.5, f32[3,256]{1,0:T(4,128)} %pos_ref.1, s32[2,3]{1,0:T(2,128)} %blk_ref.1, f32[2,16]{1,0:T(2,128)} %gam_ref.1, f32[2,2,512]{2,1,0:T(2,128)} %gains_ref.1, f32[1,512]{1,0:T(1,128)} %bitcast.3, f32[1,512]{1,0:T(1,128)} %bitcast.4, ...), custom_call_target="tpu_custom_call" | custom-call | tf_op jit(solution)/shard_map/pallas_call | solution.py:453
  43.0 1.3 %copy.19 = f32[3,256]{1,0:T(4,128)} copy(f32[3,256]{1,0:T(4,128)} %get-tuple-element.5) | data formatting | bytes 6144
